TPU v7x, 32 devices: a whole 2x2x4 slice. The times are simulated.
32 devices in a mesh: layer: 8 (over z, core), lat: 4 (over y, x).
Axes of the slice: x: 2, y: 2, z: 4, core: 2. Of those that a mesh axis runs over, the one named last changes fastest.
Arguments:
- trace_down: float32 [8, 1024, 128], P('layer', 'lat'), may hold values from -6 to 6
- trace_up: float32 [8, 1024, 128], P('layer', 'lat'), may hold values from -6 to 6
- trans_down: float32 [8, 2, 1024, 4, 128], P('layer', None, 'lat'), may hold values from -0.1875 to 0.1875
- refl_down: float32 [8, 2, 1024, 4, 128], P('layer', None, 'lat'), may hold values from -0.0625 to 0.0625
- trans_up: float32 [8, 2, 1024, 4, 128], P('layer', None, 'lat'), may hold values from -0.1875 to 0.1875
- refl_up: float32 [8, 2, 1024, 4, 128], P('layer', None, 'lat'), may hold values from -0.0625 to 0.0625
- tile_cols: int32 [8, 4, 8, 4], P('layer', None, 'lat'), may hold values from -2 to 9, as said below
- source_down: float32 [1024, 128], P('lat'), may hold values from -6 to 6
- source_up: float32 [1024, 128], P('lat'), may hold values from -6 to 6
- source_layer: int32 [64], replicated, may hold values from 0 to 7
Outputs:
- swept_down: float32 [8, 1024, 128], P('layer', 'lat')
- swept_up: float32 [8, 1024, 128], P('layer', 'lat')
Inputs may be any that keep to these rules, and one draw needn't show every extreme that they name: `tile_cols`: for row tile i of each layer and operator, the 4 entries are i - 2, then two different ones of i - 1, i, i + 1 in either order, then i + 2.
All inputs are finite; a program needn't handle non-finite values.
Results may differ from a plain program's by a relative error of at most 0.00015.
Values sent between devices are 32-bit elements; how exact they have to be, the bound alone decides.
A program may use at most 64 MiB of HBM per device.

v0:
```python
import functools

import jax
import jax.numpy as jnp
from jax import lax
from jax.experimental import pallas as pl
from jax.experimental.pallas import tpu as pltpu
from jax.sharding import PartitionSpec as P

TICKS = 5
OWN, PARTNER, FAR = 0, 1, 2
OPS = ((0, 3), (1, 2))
MESH = pl.DeviceIdType.MESH


def kernel(
    layers,
    lats,
    sl_ref,
    tc_ref,
    td_ref,
    tu_ref,
    sd_ref,
    su_ref,
    g0_ref,
    g1_ref,
    g2_ref,
    g3_ref,
    od_ref,
    ou_ref,
    gbuf,
    lhs,
    xb,
    acc,
    inj,
    tx,
    rx,
    g_sem,
    tx_sem,
    relay_sem,
    rx_sem,
):
    tile = td_ref.shape[1]
    width = td_ref.shape[2]
    half = width // 2
    quarter = width // 4
    nsrc = sl_ref.shape[0]
    layer = lax.axis_index("layer")
    lat = lax.axis_index("lat")
    par = lax.rem(lat, 2)
    partner = lat + 1 - 2 * par
    relay_to = lat + 2 - 4 * par
    relay_from = lat - 2 + 4 * par
    has_relay_to = jnp.logical_and(relay_to >= 0, relay_to < lats)
    has_far = jnp.logical_and(relay_from >= 0, relay_from < lats)
    has_src = (layer > 0, layer < layers - 1)
    has_dst = (layer < layers - 1, layer > 0)
    dst_layer = (layer + 1, layer - 1)
    sgn = 1 - 2 * par

    g_copies = [
        pltpu.make_async_copy(ref, gbuf.at[op], g_sem.at[op])
        for op, ref in enumerate((g0_ref, g1_ref, g2_ref, g3_ref))
    ]
    for copy in g_copies:
        copy.start()

    barrier = pltpu.get_barrier_semaphore()
    count = jnp.int32(0)
    for d in range(2):
        for other in (lat, partner):

            @pl.when(has_dst[d])
            def _(d=d, other=other):
                pl.semaphore_signal(
                    barrier, inc=1, device_id=(dst_layer[d], other), device_id_type=MESH
                )

        count = count + jnp.where(has_dst[d], 2, 0)

    @pl.when(has_relay_to)
    def _():
        pl.semaphore_signal(barrier, inc=1, device_id=(layer, relay_to), device_id_type=MESH)

    @pl.when(has_far)
    def _():
        pl.semaphore_signal(barrier, inc=1, device_id=(layer, relay_from), device_id_type=MESH)

    count = count + jnp.where(has_relay_to, 1, 0) + jnp.where(has_far, 1, 0)

    lane = lax.broadcasted_iota(jnp.int32, (tile, width), 1)
    first = lax.rem(lane, half) < quarter
    real = lane < half

    def pack(t0, t1):
        return (
            jnp.where(first, t0, pltpu.roll(t1, quarter, 1)),
            jnp.where(first, pltpu.roll(t0, width - quarter, 1), t1),
        )

    def unpack(p0, p1):
        return (
            jnp.where(first, p0, pltpu.roll(p1, quarter, 1)),
            jnp.where(first, pltpu.roll(p0, width - quarter, 1), p1),
        )

    for d, ref in enumerate((td_ref, tu_ref)):
        p0, p1 = pack(ref[0], ref[1])
        tx[0, d] = p0
        tx[1, d] = p1

    def send_copy(slot, g, d, piece):
        return pltpu.make_async_remote_copy(
            src_ref=tx.at[g, d],
            dst_ref=rx.at[slot, g, d, piece],
            send_sem=tx_sem.at[g, d, piece],
            recv_sem=rx_sem.at[slot, g, d, piece],
            device_id=(dst_layer[d], partner if piece == PARTNER else lat),
            device_id_type=MESH,
        )

    def relay_copy(slot, g, d):
        return pltpu.make_async_remote_copy(
            src_ref=rx.at[slot, g, d, PARTNER],
            dst_ref=rx.at[slot, g, d, FAR],
            send_sem=relay_sem.at[g, d],
            recv_sem=rx_sem.at[slot, g, d, FAR],
            device_id=(layer, relay_to),
            device_id_type=MESH,
        )

    def send(slot, g):
        for d in range(2):

            @pl.when(has_dst[d])
            def _(d=d):
                send_copy(slot, g, d, PARTNER).start()
                send_copy(slot, g, d, OWN).start()

    def wait_send(slot, g):
        for d in range(2):

            @pl.when(has_dst[d])
            def _(d=d):
                send_copy(slot, g, d, PARTNER).wait_send()
                send_copy(slot, g, d, OWN).wait_send()

    pl.semaphore_wait(barrier, count)
    for g in range(2):
        send(0, g)

    xb[...] = jnp.zeros_like(xb)
    row = lax.broadcasted_iota(jnp.int32, (8, width), 1)
    row = lax.rem(row, half)
    hits = jnp.zeros((8, width), jnp.float32)
    for s in range(nsrc):
        hit = jnp.where(sl_ref[s] == layer, 1.0, 0.0).astype(jnp.float32)
        hits = jnp.where(row == s, hit, hits)
    hit_row = hits[0:1] > 0.5
    for d, ref in enumerate((sd_ref, su_ref)):
        p0, p1 = pack(jnp.where(hit_row, ref[0], 0.0), jnp.where(hit_row, ref[1], 0.0))
        inj[0, d] = p0
        inj[1, d] = p1

    for copy in g_copies:
        copy.wait()
    for d in range(2):
        for i in range(2):
            ia = i + par - 2 * i * par
            base = ia * (4 * tile)
            for j, op in enumerate(OPS[d]):
                at = lat * 2 + ia
                c1 = (tc_ref[op, ia, 1] - at) * sgn
                c2 = (tc_ref[op, ia, 2] - at) * sgn
                for c in range(2):
                    w1 = gbuf[op, c, pl.ds(base + 1, tile, stride=4), :]
                    w2 = gbuf[op, c, pl.ds(base + 2, tile, stride=4), :]
                    for slot in range(5):
                        if slot == 0:
                            val = gbuf[op, c, pl.ds(base + 3 * par, tile, stride=4), :]
                        elif slot == 4:
                            val = gbuf[op, c, pl.ds(base + 3 - 3 * par, tile, stride=4), :]
                        else:
                            val = jnp.where(c1 == slot - 2, w1, jnp.where(c2 == slot - 2, w2, 0.0))
                        hi = val.astype(jnp.bfloat16)
                        lo = (val - hi.astype(jnp.float32)).astype(jnp.bfloat16)
                        cols = pl.ds(slot * 2 * tile + c * tile, tile)
                        lhs[d, i, pl.ds(j * tile, tile), cols] = hi
                        lhs[d, i, pl.ds((2 + j) * tile, tile), cols] = lo

    def build(slot, g, d, piece, at):
        packed = rx[slot, g, d, piece]
        hi = packed.astype(jnp.bfloat16).astype(jnp.float32)
        lo = packed - hi
        for h in range(2):
            if h == 0:
                x = jnp.where(first, hi, pltpu.roll(lo, quarter, 1))
            else:
                x = jnp.where(first, pltpu.roll(lo, width - quarter, 1), hi)
            other = pltpu.roll(x, half, 1)
            xs = jnp.where(real, -other, other)
            place = (at + h + par - 2 * h * par) * (2 * tile)
            xb[d, pl.ds(place, tile), :] = x.astype(jnp.bfloat16)
            xb[d, pl.ds(place + tile, tile), :] = xs.astype(jnp.bfloat16)

    def wait_recv(slot, g, d, piece):
        if piece == FAR:
            relay_copy(slot, g, d).wait_recv()
        else:
            send_copy(slot, g, d, piece).wait_recv()

    def relay(slot, g):
        for d in range(2):

            @pl.when(has_src[d])
            def _(d=d):
                wait_recv(slot, g, d, PARTNER)

                @pl.when(has_relay_to)
                def _():
                    relay_copy(slot, g, d).start()

    def products(slots_of, tiles_of):
        sums = [[None, None], [None, None]]
        for i in range(2):
            s0, s1 = slots_of[i]
            e0 = tiles_of[i]
            for d in range(2):
                y = jnp.dot(
                    lhs[d, i, :, pl.ds(s0 * 2 * tile, (s1 - s0) * 2 * tile)],
                    xb[d, pl.ds(e0 * 2 * tile, (s1 - s0) * 2 * tile), :],
                    preferred_element_type=jnp.float32,
                )
                for j in range(2):
                    part = y[j * tile : (j + 1) * tile] + y[(2 + j) * tile : (3 + j) * tile]
                    sums[i][j] = part if d == 0 else sums[i][j] + part
        return sums

    def near(slot, g):
        for d in range(2):

            @pl.when(has_src[d])
            def _(d=d):
                wait_recv(slot, g, d, OWN)
                build(slot, g, d, OWN, 2)
                build(slot, g, d, PARTNER, 4)

        sums = products(((2, 5), (1, 5)), (2, 2))
        for i in range(2):
            for j in range(2):
                acc[i, j] = sums[i][j]

    swap = jnp.logical_xor(first, par == 1)

    def far(tick, slot, g):
        for d in range(2):

            @pl.when(jnp.logical_and(has_src[d], has_far))
            def _(d=d):
                wait_recv(slot, g, d, FAR)
                build(slot, g, d, FAR, 0)

        sums = products(((0, 2), (0, 1)), (0, 1))
        for d in range(2):

            @pl.when(jnp.logical_and(has_src[d], has_relay_to))
            def _(d=d):
                relay_copy(slot, g, d).wait_send()

        wait_send(slot, g)
        for j in range(2):
            s0 = sums[0][j] + acc[0, j]
            s1 = sums[1][j] + acc[1, j]
            ya = jnp.where(swap, s0, s1)
            other = jnp.where(first, pltpu.roll(s0, width - quarter, 1), pltpu.roll(s0, quarter, 1))
            other1 = jnp.where(first, pltpu.roll(s1, width - quarter, 1), pltpu.roll(s1, quarter, 1))
            tx[g, j] = ya + jnp.where(swap, other, other1) + inj[g, j]

        @pl.when(tick < TICKS - 1)
        def _():
            send(1 - slot, g)

    relay(0, 0)

    def tick_body(tick, carry):
        slot = lax.rem(tick, 2)
        near(slot, 0)
        relay(slot, 1)
        far(tick, slot, 0)
        near(slot, 1)

        @pl.when(tick < TICKS - 1)
        def _():
            relay(1 - slot, 0)

        far(tick, slot, 1)
        return carry

    lax.fori_loop(0, TICKS, tick_body, 0)
    for d, ref in enumerate((od_ref, ou_ref)):
        t0, t1 = unpack(tx[0, d], tx[1, d])
        ref[0] = t0
        ref[1] = t1


def on_device(
    layers,
    lats,
    trace_down,
    trace_up,
    trans_down,
    refl_down,
    trans_up,
    refl_up,
    tile_cols,
    source_down,
    source_up,
    source_layer,
):
    tile = trans_down.shape[-1]
    rows, width = trace_down.shape[1], trace_down.shape[2]
    row_tiles = rows // tile
    assert row_tiles == 2 and lats % 2 == 0
    strip = (row_tiles, tile, width)
    vmem = pl.BlockSpec(memory_space=pltpu.VMEM)
    smem = pl.BlockSpec(memory_space=pltpu.SMEM)
    hbm = pl.BlockSpec(memory_space=pl.ANY)
    greens = [g.reshape(2, rows * 4, tile) for g in (trans_down, refl_down, trans_up, refl_up)]
    out = jax.ShapeDtypeStruct(strip, jnp.float32)
    down, up = pl.pallas_call(
        functools.partial(kernel, layers, lats),
        out_shape=(out, out),
        in_specs=[smem, smem, vmem, vmem, vmem, vmem, hbm, hbm, hbm, hbm],
        out_specs=(vmem, vmem),
        scratch_shapes=[
            pltpu.VMEM((4, 2, rows * 4, tile), jnp.float32),
            pltpu.VMEM((2, 2, 4 * tile, 10 * tile), jnp.bfloat16),
            pltpu.VMEM((2, 12 * tile, width), jnp.bfloat16),
            pltpu.VMEM((2, 2, tile, width), jnp.float32),
            pltpu.VMEM((2, 2, tile, width), jnp.float32),
            pltpu.VMEM((2, 2, tile, width), jnp.float32),
            pltpu.VMEM((2, 2, 2, 3, tile, width), jnp.float32),
            pltpu.SemaphoreType.DMA((4,)),
            pltpu.SemaphoreType.DMA((2, 2, 2)),
            pltpu.SemaphoreType.DMA((2, 2)),
            pltpu.SemaphoreType.DMA((2, 2, 2, 3)),
        ],
        compiler_params=pltpu.CompilerParams(
            collective_id=0, has_side_effects=True, vmem_limit_bytes=40 * 1024 * 1024
        ),
    )(
        source_layer,
        tile_cols[0],
        trace_down.reshape(strip),
        trace_up.reshape(strip),
        source_down.reshape(strip),
        source_up.reshape(strip),
        *greens,
    )
    return (down.reshape(1, rows, width), up.reshape(1, rows, width))


def solution(mesh):
    in_specs = (
        P("layer", "lat", None),
        P("layer", "lat", None),
        P("layer", None, "lat", None, None),
        P("layer", None, "lat", None, None),
        P("layer", None, "lat", None, None),
        P("layer", None, "lat", None, None),
        P("layer", None, "lat", None),
        P("lat", None),
        P("lat", None),
        P(),
    )
    out_specs = (P("layer", "lat", None), P("layer", "lat", None))
    return jax.shard_map(
        functools.partial(on_device, mesh.shape["layer"], mesh.shape["lat"]),
        mesh=mesh,
        in_specs=in_specs,
        out_specs=out_specs,
        check_vma=False,
    )
```

profile of v0, /device:TPU:21, one launch (start us, length us, event | category | flops | bytes accessed | tf_op | source)
XLA Modules:
  0.0 71.6 jit_solution(1409351893501433872)
XLA Ops:
  0.6 0.0 copy-start.8
  0.6 0.0 copy-start.9
  0.7 0.7 copy-done.8
  1.3 0.0 copy-done.9
  1.3 0.0 copy-start
  1.3 1.2 %copy-done = f32[1,2,256,4,128]{4,3,2,1,0:T(4,128)S(1)} copy-done((f32[1,2,256,4,128]{4,3,2,1,0:T(4,128)S(1)}, f32[1,2,256,4,128]{4,3,2,1,0:T(4,128)}, u32[]{:S(2)}) %copy-start) | copy-done | bytes 1048600
  2.5 0.0 copy-start.1
  2.6 1.2 %copy-done.1 = f32[1,2,256,4,128]{4,3,2,1,0:T(4,128)S(1)} copy-done((f32[1,2,256,4,128]{4,3,2,1,0:T(4,128)S(1)}, f32[1,2,256,4,128]{4,3,2,1,0:T(4,128)}, u32[]{:S(2)}) %copy-start.1) | copy-done | bytes 1048600
  3.8 0.0 copy-start.2
  3.8 1.2 %copy-done.2 = f32[1,2,256,4,128]{4,3,2,1,0:T(4,128)S(1)} copy-done((f32[1,2,256,4,128]{4,3,2,1,0:T(4,128)S(1)}, f32[1,2,256,4,128]{4,3,2,1,0:T(4,128)}, u32[]{:S(2)}) %copy-start.2) | copy-done | bytes 1048600
  5.0 0.0 copy-start.3
  5.0 1.2 %copy-done.3 = f32[1,2,256,4,128]{4,3,2,1,0:T(4,128)S(1)} copy-done((f32[1,2,256,4,128]{4,3,2,1,0:T(4,128)S(1)}, f32[1,2,256,4,128]{4,3,2,1,0:T(4,128)}, u32[]{:S(2)}) %copy-start.3) | copy-done | bytes 1048600
  6.2 0.0 copy-start.4
  6.2 0.9 %copy-done.4 = f32[1,256,128]{2,1,0:T(8,128)S(1)} copy-done((f32[1,256,128]{2,1,0:T(8,128)S(1)}, f32[1,256,128]{2,1,0:T(8,128)}, u32[]{:S(2)}) %copy-start.4) | copy-done | bytes 131096
  7.1 0.0 copy-start.5
  7.1 0.9 %copy-done.5 = f32[1,256,128]{2,1,0:T(8,128)S(1)} copy-done((f32[1,256,128]{2,1,0:T(8,128)S(1)}, f32[1,256,128]{2,1,0:T(8,128)}, u32[]{:S(2)}) %copy-start.5) | copy-done | bytes 131096
  8.0 0.0 copy-start.6
  8.0 0.9 %copy-done.6 = f32[256,128]{1,0:T(8,128)S(1)} copy-done((f32[256,128]{1,0:T(8,128)S(1)}, f32[256,128]{1,0:T(8,128)}, u32[]{:S(2)}) %copy-start.6) | copy-done | bytes 131096
  8.9 0.0 copy-start.7
  8.9 0.9 %copy-done.7 = f32[256,128]{1,0:T(8,128)S(1)} copy-done((f32[256,128]{1,0:T(8,128)S(1)}, f32[256,128]{1,0:T(8,128)}, u32[]{:S(2)}) %copy-start.7) | copy-done | bytes 131096
  9.8 60.4 %shard_map.113 = (f32[2,128,128]{2,1,0:T(8,128)S(1)}, f32[2,128,128]{2,1,0:T(8,128)S(1)}) custom-call(s32[64]{0:T(128)S(1)} %copy-done.9, s32[4,2,4]{2,1,0:T(2,128)S(1)} %bitcast.21, f32[2,128,128]{2,1,0:T(8,128)S(1)} %bitcast.15, f32[2,128,128]{2,1,0:T(8,128)S(1)} %bitcast.16, f32[2,128,128]{2,1,0:T(8,128)S(1)} %bitcast.17, f32[2,128,128]{2,1,0:T(8,128)S(1)} %bitcast.18, ...), custom_call_target="tpu_custom_call" | custom-call | tf_op jit(solution)/shard_map/pallas_call | solution.py:330
  70.3 0.7 copy.14
  70.9 0.7 copy.15
Async XLA Ops:
  0.6 0.7 copy-start.8
  0.6 0.7 copy-start.9
  1.3 1.2 %copy-start = (f32[1,2,256,4,128]{4,3,2,1,0:T(4,128)S(1)}, f32[1,2,256,4,128]{4,3,2,1,0:T(4,128)}, u32[]{:S(2)}) copy-start(f32[1,2,256,4,128]{4,3,2,1,0:T(4,128)} %param.12) | copy-start | bytes 3145732
  2.5 1.2 %copy-start.1 = (f32[1,2,256,4,128]{4,3,2,1,0:T(4,128)S(1)}, f32[1,2,256,4,128]{4,3,2,1,0:T(4,128)}, u32[]{:S(2)}) copy-start(f32[1,2,256,4,128]{4,3,2,1,0:T(4,128)} %param.13) | copy-start | bytes 3145732
  3.8 1.2 %copy-start.2 = (f32[1,2,256,4,128]{4,3,2,1,0:T(4,128)S(1)}, f32[1,2,256,4,128]{4,3,2,1,0:T(4,128)}, u32[]{:S(2)}) copy-start(f32[1,2,256,4,128]{4,3,2,1,0:T(4,128)} %param.14) | copy-start | bytes 3145732
  5.0 1.2 %copy-start.3 = (f32[1,2,256,4,128]{4,3,2,1,0:T(4,128)S(1)}, f32[1,2,256,4,128]{4,3,2,1,0:T(4,128)}, u32[]{:S(2)}) copy-start(f32[1,2,256,4,128]{4,3,2,1,0:T(4,128)} %param.15) | copy-start | bytes 3145732
  6.2 0.9 %copy-start.4 = (f32[1,256,128]{2,1,0:T(8,128)S(1)}, f32[1,256,128]{2,1,0:T(8,128)}, u32[]{:S(2)}) copy-start(f32[1,256,128]{2,1,0:T(8,128)} %param.10) | copy-start | bytes 393220
  7.1 0.9 %copy-start.5 = (f32[1,256,128]{2,1,0:T(8,128)S(1)}, f32[1,256,128]{2,1,0:T(8,128)}, u32[]{:S(2)}) copy-start(f32[1,256,128]{2,1,0:T(8,128)} %param.11) | copy-start | bytes 393220
  8.0 0.9 %copy-start.6 = (f32[256,128]{1,0:T(8,128)S(1)}, f32[256,128]{1,0:T(8,128)}, u32[]{:S(2)}) copy-start(f32[256,128]{1,0:T(8,128)} %param.17) | copy-start | bytes 393220
  8.9 0.9 %copy-start.7 = (f32[256,128]{1,0:T(8,128)S(1)}, f32[256,128]{1,0:T(8,128)}, u32[]{:S(2)}) copy-start(f32[256,128]{1,0:T(8,128)} %param.18) | copy-start | bytes 393220
where the time goes:
time: 72 us; the launch traced here: 71.6 us
  Pallas kernels  60.4 us (84%)
  local copies, waits for them, and re-layouts  10.5 us (15%)
    pallas_call x1, Pallas kernels, on_device(): pl.pallas_call(functools.partial(kernel, layers, lats), out_shape=(out, o...  60.4 us
    unnamed x22, local copies, waits for them, and re-layouts  10.5 us

commit v1 on v0

--- a/solution.py
+++ b/solution.py
@@ -9,6 +9,7 @@
 
 TICKS = 5
 OWN, PARTNER, FAR = 0, 1, 2
+CHUNKS = 2
 OPS = ((0, 3), (1, 2))
 MESH = pl.DeviceIdType.MESH
 
@@ -28,6 +29,7 @@
     g3_ref,
     od_ref,
     ou_ref,
+    raw,
     gbuf,
     lhs,
     xb,
@@ -35,6 +37,7 @@
     inj,
     tx,
     rx,
+    raw_sem,
     g_sem,
     tx_sem,
     relay_sem,
@@ -58,6 +61,12 @@
     dst_layer = (layer + 1, layer - 1)
     sgn = 1 - 2 * par
 
+    raw_copies = [
+        pltpu.make_async_copy(ref, raw.at[n], raw_sem.at[n])
+        for n, ref in enumerate((td_ref, tu_ref, sd_ref, su_ref))
+    ]
+    for copy in raw_copies:
+        copy.start()
     g_copies = [
         pltpu.make_async_copy(ref, gbuf.at[op], g_sem.at[op])
         for op, ref in enumerate((g0_ref, g1_ref, g2_ref, g3_ref))
@@ -104,27 +113,32 @@
             jnp.where(first, pltpu.roll(p0, width - quarter, 1), p1),
         )
 
-    for d, ref in enumerate((td_ref, tu_ref)):
-        p0, p1 = pack(ref[0], ref[1])
+    for d in range(2):
+        raw_copies[d].wait()
+        p0, p1 = pack(raw[d, 0], raw[d, 1])
         tx[0, d] = p0
         tx[1, d] = p1
 
-    def send_copy(slot, g, d, piece):
+    chunk_rows = tile // CHUNKS
+
+    def send_copy(slot, g, d, piece, n):
+        rows = pl.ds(n * chunk_rows, chunk_rows)
         return pltpu.make_async_remote_copy(
-            src_ref=tx.at[g, d],
-            dst_ref=rx.at[slot, g, d, piece],
-            send_sem=tx_sem.at[g, d, piece],
-            recv_sem=rx_sem.at[slot, g, d, piece],
+            src_ref=tx.at[g, d, rows],
+            dst_ref=rx.at[slot, g, d, piece, rows],
+            send_sem=tx_sem.at[g, d, piece, n],
+            recv_sem=rx_sem.at[slot, g, d, piece, n],
             device_id=(dst_layer[d], partner if piece == PARTNER else lat),
             device_id_type=MESH,
         )
 
-    def relay_copy(slot, g, d):
+    def relay_copy(slot, g, d, n):
+        rows = pl.ds(n * chunk_rows, chunk_rows)
         return pltpu.make_async_remote_copy(
-            src_ref=rx.at[slot, g, d, PARTNER],
-            dst_ref=rx.at[slot, g, d, FAR],
-            send_sem=relay_sem.at[g, d],
-            recv_sem=rx_sem.at[slot, g, d, FAR],
+            src_ref=rx.at[slot, g, d, PARTNER, rows],
+            dst_ref=rx.at[slot, g, d, FAR, rows],
+            send_sem=relay_sem.at[g, d, n],
+            recv_sem=rx_sem.at[slot, g, d, FAR, n],
             device_id=(layer, relay_to),
             device_id_type=MESH,
         )
@@ -134,16 +148,18 @@
 
             @pl.when(has_dst[d])
             def _(d=d):
-                send_copy(slot, g, d, PARTNER).start()
-                send_copy(slot, g, d, OWN).start()
+                for piece in (PARTNER, OWN):
+                    for n in range(CHUNKS):
+                        send_copy(slot, g, d, piece, n).start()
 
     def wait_send(slot, g):
         for d in range(2):
 
             @pl.when(has_dst[d])
             def _(d=d):
-                send_copy(slot, g, d, PARTNER).wait_send()
-                send_copy(slot, g, d, OWN).wait_send()
+                for piece in (PARTNER, OWN):
+                    for n in range(CHUNKS):
+                        send_copy(slot, g, d, piece, n).wait_send()
 
     pl.semaphore_wait(barrier, count)
     for g in range(2):
@@ -157,8 +173,11 @@
         hit = jnp.where(sl_ref[s] == layer, 1.0, 0.0).astype(jnp.float32)
         hits = jnp.where(row == s, hit, hits)
     hit_row = hits[0:1] > 0.5
-    for d, ref in enumerate((sd_ref, su_ref)):
-        p0, p1 = pack(jnp.where(hit_row, ref[0], 0.0), jnp.where(hit_row, ref[1], 0.0))
+    for d in range(2):
+        raw_copies[2 + d].wait()
+        p0, p1 = pack(
+            jnp.where(hit_row, raw[2 + d, 0], 0.0), jnp.where(hit_row, raw[2 + d, 1], 0.0)
+        )
         inj[0, d] = p0
         inj[1, d] = p1
 
@@ -204,37 +223,31 @@
             xb[d, pl.ds(place + tile, tile), :] = xs.astype(jnp.bfloat16)
 
     def wait_recv(slot, g, d, piece):
-        if piece == FAR:
-            relay_copy(slot, g, d).wait_recv()
-        else:
-            send_copy(slot, g, d, piece).wait_recv()
+        for n in range(CHUNKS):
+            if piece == FAR:
+                relay_copy(slot, g, d, n).wait_recv()
+            else:
+                send_copy(slot, g, d, piece, n).wait_recv()
 
     def relay(slot, g):
         for d in range(2):
 
             @pl.when(has_src[d])
             def _(d=d):
-                wait_recv(slot, g, d, PARTNER)
-
-                @pl.when(has_relay_to)
-                def _():
-                    relay_copy(slot, g, d).start()
-
-    def products(slots_of, tiles_of):
-        sums = [[None, None], [None, None]]
-        for i in range(2):
-            s0, s1 = slots_of[i]
-            e0 = tiles_of[i]
-            for d in range(2):
-                y = jnp.dot(
-                    lhs[d, i, :, pl.ds(s0 * 2 * tile, (s1 - s0) * 2 * tile)],
-                    xb[d, pl.ds(e0 * 2 * tile, (s1 - s0) * 2 * tile), :],
-                    preferred_element_type=jnp.float32,
-                )
-                for j in range(2):
-                    part = y[j * tile : (j + 1) * tile] + y[(2 + j) * tile : (3 + j) * tile]
-                    sums[i][j] = part if d == 0 else sums[i][j] + part
-        return sums
+                for n in range(CHUNKS):
+                    send_copy(slot, g, d, PARTNER, n).wait_recv()
+
+                    @pl.when(has_relay_to)
+                    def _(n=n):
+                        relay_copy(slot, g, d, n).start()
+
+    def product(d, i, slot0, slot1, e0):
+        y = jnp.dot(
+            lhs[d, i, :, pl.ds(slot0 * 2 * tile, (slot1 - slot0) * 2 * tile)],
+            xb[d, pl.ds(e0 * 2 * tile, (slot1 - slot0) * 2 * tile), :],
+            preferred_element_type=jnp.float32,
+        )
+        return [y[j * tile : (j + 1) * tile] + y[(2 + j) * tile : (3 + j) * tile] for j in range(2)]
 
     def near(slot, g):
         for d in range(2):
@@ -245,10 +258,10 @@
                 build(slot, g, d, OWN, 2)
                 build(slot, g, d, PARTNER, 4)
 
-        sums = products(((2, 5), (1, 5)), (2, 2))
         for i in range(2):
+            parts = [product(d, i, 2 - i, 5, 2) for d in range(2)]
             for j in range(2):
-                acc[i, j] = sums[i][j]
+                acc[i, j] = parts[0][j] + parts[1][j]
 
     swap = jnp.logical_xor(first, par == 1)
 
@@ -259,41 +272,35 @@
             def _(d=d):
                 wait_recv(slot, g, d, FAR)
                 build(slot, g, d, FAR, 0)
-
-        sums = products(((0, 2), (0, 1)), (0, 1))
+                for i in range(2):
+                    part = product(d, i, 0, 2 - i, i)
+                    for j in range(2):
+                        acc[i, j] += part[j]
+
         for d in range(2):
 
             @pl.when(jnp.logical_and(has_src[d], has_relay_to))
             def _(d=d):
-                relay_copy(slot, g, d).wait_send()
+                for n in range(CHUNKS):
+                    relay_copy(slot, g, d, n).wait_send()
 
         wait_send(slot, g)
         for j in range(2):
-            s0 = sums[0][j] + acc[0, j]
-            s1 = sums[1][j] + acc[1, j]
-            ya = jnp.where(swap, s0, s1)
-            other = jnp.where(first, pltpu.roll(s0, width - quarter, 1), pltpu.roll(s0, quarter, 1))
+            s0, s1 = acc[0, j], acc[1, j]
+            other0 = jnp.where(first, pltpu.roll(s0, width - quarter, 1), pltpu.roll(s0, quarter, 1))
             other1 = jnp.where(first, pltpu.roll(s1, width - quarter, 1), pltpu.roll(s1, quarter, 1))
-            tx[g, j] = ya + jnp.where(swap, other, other1) + inj[g, j]
+            tx[g, j] = jnp.where(swap, s0 + other0, s1 + other1) + inj[g, j]
 
         @pl.when(tick < TICKS - 1)
         def _():
             send(1 - slot, g)
 
-    relay(0, 0)
-
     def tick_body(tick, carry):
         slot = lax.rem(tick, 2)
-        near(slot, 0)
-        relay(slot, 1)
-        far(tick, slot, 0)
-        near(slot, 1)
-
-        @pl.when(tick < TICKS - 1)
-        def _():
-            relay(1 - slot, 0)
-
-        far(tick, slot, 1)
+        for g in range(2):
+            relay(slot, g)
+            near(slot, g)
+            far(tick, slot, g)
         return carry
 
     lax.fori_loop(0, TICKS, tick_body, 0)
@@ -324,15 +331,16 @@
     strip = (row_tiles, tile, width)
     vmem = pl.BlockSpec(memory_space=pltpu.VMEM)
     smem = pl.BlockSpec(memory_space=pltpu.SMEM)
-    hbm = pl.BlockSpec(memory_space=pl.ANY)
+    hbm = pl.BlockSpec(memory_space=pltpu.HBM)
     greens = [g.reshape(2, rows * 4, tile) for g in (trans_down, refl_down, trans_up, refl_up)]
     out = jax.ShapeDtypeStruct(strip, jnp.float32)
     down, up = pl.pallas_call(
         functools.partial(kernel, layers, lats),
         out_shape=(out, out),
-        in_specs=[smem, smem, vmem, vmem, vmem, vmem, hbm, hbm, hbm, hbm],
+        in_specs=[smem, smem] + [hbm] * 8,
         out_specs=(vmem, vmem),
         scratch_shapes=[
+            pltpu.VMEM((4,) + strip, jnp.float32),
             pltpu.VMEM((4, 2, rows * 4, tile), jnp.float32),
             pltpu.VMEM((2, 2, 4 * tile, 10 * tile), jnp.bfloat16),
             pltpu.VMEM((2, 12 * tile, width), jnp.bfloat16),
@@ -341,12 +349,13 @@
             pltpu.VMEM((2, 2, tile, width), jnp.float32),
             pltpu.VMEM((2, 2, 2, 3, tile, width), jnp.float32),
             pltpu.SemaphoreType.DMA((4,)),
-            pltpu.SemaphoreType.DMA((2, 2, 2)),
-            pltpu.SemaphoreType.DMA((2, 2)),
-            pltpu.SemaphoreType.DMA((2, 2, 2, 3)),
+            pltpu.SemaphoreType.DMA((4,)),
+            pltpu.SemaphoreType.DMA((2, 2, 2, CHUNKS)),
+            pltpu.SemaphoreType.DMA((2, 2, CHUNKS)),
+            pltpu.SemaphoreType.DMA((2, 2, 2, 3, CHUNKS)),
         ],
         compiler_params=pltpu.CompilerParams(
-            collective_id=0, has_side_effects=True, vmem_limit_bytes=40 * 1024 * 1024
+            collective_id=0, has_side_effects=True
         ),
     )(
         source_layer,

time: 72 us -> 54.7 us (0.76)
  Pallas kernels: 60.4 us -> 51.6 us
  local copies, waits for them, and re-layouts: 10.5 us -> 2.26 us
    pallas_call x1, Pallas kernels: 60.4 us -> 51.6 us  [on_device(): pl.pallas_call(functools.partial(kernel, layers, lats), out_shape=(out, o...]
    unnamed x22 -> x4, local copies, waits for them, and re-layouts: 10.5 us -> 2.26 us
where the time goes in v1:
time: 54.7 us; the launch traced here: 54.5 us
  Pallas kernels  51.6 us (94%)
  local copies, waits for them, and re-layouts  2.26 us (4%)
  between operations  0.65 us (1%)
    pallas_call x1, Pallas kernels, on_device(): pl.pallas_call(functools.partial(kernel, layers, lats), out_shape=(out, o...  51.6 us
    unnamed x4, local copies, waits for them, and re-layouts  2.26 us

profile of v1, /device:TPU:21, one launch (start us, length us, event | category | flops | bytes accessed | tf_op | source)
XLA Modules:
  0.0 54.5 jit_solution(1791446698473703272)
XLA Ops:
  0.6 51.6 %shard_map.113 = (f32[2,128,128]{2,1,0:T(8,128)}, f32[2,128,128]{2,1,0:T(8,128)}) custom-call(s32[64]{0:T(128)} %sl_ref.1, s32[4,2,4]{2,1,0:T(2,128)} %bitcast.21, f32[2,128,128]{2,1,0:T(8,128)} %bitcast.15, f32[2,128,128]{2,1,0:T(8,128)} %bitcast.16, f32[2,128,128]{2,1,0:T(8,128)} %bitcast.17, f32[2,128,128]{2,1,0:T(8,128)} %bitcast.18, ...), custom_call_target="tpu_custom_call" | custom-call | tf_op jit(solution)/shard_map/pallas_call | solution.py:337
  52.2 0.0 copy-start
  52.2 1.6 %copy.14 = f32[1,256,128]{2,1,0:T(8,128)} copy(f32[1,256,128]{2,1,0:T(8,128)} %bitcast.20) | data formatting | bytes 262144
  53.9 0.0 copy-done
  53.9 0.7 %copy.15 = f32[1,256,128]{2,1,0:T(8,128)} copy(f32[1,256,128]{2,1,0:T(8,128)S(1)} %bitcast.19) | data formatting | bytes 262144
Async XLA Ops:
  52.2 1.6 %copy-start = (f32[2,128,128]{2,1,0:T(8,128)S(1)}, f32[2,128,128]{2,1,0:T(8,128)}, u32[]{:S(2)}) copy-start(f32[2,128,128]{2,1,0:T(8,128)} %get-tuple-element.5) | copy-start | bytes 393220
